TPU v7x, 256 devices: a whole 4x4x8 slice. The times are simulated.
256 devices in a mesh: chan: 64 (over y, z, core), hour: 4 (over x).
Axes of the slice: x: 4, y: 4, z: 8, core: 2. Of those that a mesh axis runs over, the one named last changes fastest.
Arguments:
- spectra: bfloat16 [8, 2, 8192, 2560], P('hour', None, 'chan'), may hold values from -34 to 34, as said below
- partner_lists: int32 [64, 4], replicated, may hold values from -1 to 63, as said below
- partner_counts: int32 [64], replicated, may hold values from 2 to 4, as said below
Outputs:
- stacks: float32 [256, 8, 128, 256], P(('chan', 'hour'))
Inputs may be any that keep to these rules, and one draw needn't show every extreme that they name: The spectra are finite and bounded. `partner_lists`: row s lists distinct channel blocks, the first being s itself; entries from position partner_counts[s] on are -1. Within their counts, every block is listed by at most 4 rows, and some block by exactly 4. `partner_counts`: some row has exactly 4 partners.
All inputs are finite; a program needn't handle non-finite values.
Results may differ from a plain program's by a relative error of at most 0.0046.
Values may be sent and summed in bfloat16 or wider, within the bound.
A program may use at most 128 MiB of HBM per device.

v0:
```python
import math
import jax
import jax.numpy as jnp
from jax import lax
from jax.sharding import PartitionSpec as P

VS = 8
F0 = 64
NWIN = 8192
SMOOTH = 129
LAGS = 256


def whiten(real_part, imag_part):
    amplitude = jnp.sqrt(real_part * real_part + imag_part * imag_part)
    window_shape = (1,) * (amplitude.ndim - 1) + (SMOOTH,)
    padding = ((0, 0),) * (amplitude.ndim - 1) + ((SMOOTH // 2, SMOOTH // 2),)
    summed = lax.reduce_window(
        amplitude,
        jnp.zeros((), amplitude.dtype),
        lax.add,
        window_shape,
        (1,) * amplitude.ndim,
        padding,
    )
    denominator = summed / SMOOTH + 1e-06
    return (
        (real_part / denominator).astype(jnp.bfloat16),
        (imag_part / denominator).astype(jnp.bfloat16),
    )


def lag_table(band_bins):
    freq_index = jnp.arange(band_bins, dtype=jnp.int32)[:, None] + F0
    lag_index = jnp.arange(LAGS, dtype=jnp.int32)[None, :] - LAGS // 2
    lag_index = jnp.where(lag_index < 0, lag_index + NWIN, lag_index)
    phase_index = freq_index * lag_index % NWIN
    phase_angle = phase_index.astype(jnp.float32) * (2.0 * math.pi / NWIN)
    return jnp.concatenate([jnp.cos(phase_angle), -jnp.sin(phase_angle)], 0).astype(jnp.bfloat16)


def slot_onehot(partner_lists, partner_counts, receiver):
    offsets = jnp.arange(partner_lists.shape[1], dtype=jnp.int32)
    listed = (offsets[None, :] < partner_counts[:, None]) & (partner_lists == receiver)
    member = jnp.any(listed, axis=1)
    slot_rank = jnp.cumsum(member.astype(jnp.int32)) - 1
    slots = jnp.arange(partner_lists.shape[1], dtype=jnp.int32)
    return member[None, :] & (slot_rank[None, :] == slots[:, None])


def shards(spectra, partner_lists, partner_counts):
    windows, _, block_chans, band_bins = spectra.shape
    block_count = lax.axis_size("chan")
    hour_count = lax.axis_size("hour")
    values = spectra.astype(jnp.float32)
    white_re, white_im = whiten(values[:, 0], values[:, 1])
    stride = block_chans // VS
    local_sources = jnp.stack([white_re[:, ::stride, :], white_im[:, ::stride, :]], 1)
    local_sources = jnp.transpose(local_sources, (2, 0, 1, 3))
    receiver = lax.axis_index("chan")
    onehot = slot_onehot(partner_lists, partner_counts, receiver).astype(jnp.bfloat16)
    slot_total = onehot.shape[0]
    gathered = lax.all_gather(local_sources, "chan", axis=0, tiled=True)
    flattened = gathered.reshape(block_count, -1)
    chosen = jnp.dot(onehot, flattened, preferred_element_type=jnp.float32)
    chosen = chosen.reshape(slot_total, VS, windows, 2, band_bins)
    table_values = lag_table(band_bins)
    norm_scale = 1.0 / math.sqrt(4.0 * band_bins * windows * hour_count)

    def one_slot(source):
        cross_re = jnp.zeros((VS, block_chans, band_bins), jnp.float32)
        cross_im = jnp.zeros((VS, block_chans, band_bins), jnp.float32)
        for window in range(windows):
            src_real = source[:, window, 0][:, None, :]
            src_imag = source[:, window, 1][:, None, :]
            recv_real = white_re[window][None, :, :]
            recv_imag = white_im[window][None, :, :]
            cross_re = cross_re + src_real * recv_real + src_imag * recv_imag
            cross_im = cross_im + src_imag * recv_real - src_real * recv_imag
        cross = (
            jnp.concatenate([cross_re, cross_im], -1)
            .astype(jnp.bfloat16)
            .reshape(VS * block_chans, 2 * band_bins)
        )
        lagged = jnp.dot(cross, table_values, preferred_element_type=jnp.float32) * norm_scale
        return lagged.reshape(VS, block_chans, LAGS)

    partial_stacks = lax.map(one_slot, chosen)
    summed_hours = lax.psum(partial_stacks, "hour")
    share = slot_total // hour_count
    return lax.dynamic_slice_in_dim(summed_hours, lax.axis_index("hour") * share, share, 0)


def solution(mesh):
    return jax.shard_map(
        shards,
        mesh=mesh,
        in_specs=(P("hour", None, "chan", None), P(), P()),
        out_specs=P(("chan", "hour"), None, None, None),
        check_vma=False,
    )
```

profile of v0, /device:TPU:1, one launch (start us, length us, event | category | flops | bytes accessed | tf_op | source)
XLA Modules:
  0.0 464.1 jit_solution(17760751546049418316)
XLA Ops:
  6.5 3.2 copy.26
  10.1 2.3 copy-done
  13.3 129.2 %reduce_window.7 = f32[2,128,2560]{1,2,0:T(8,128)} reduce-window(f32[2,128,2560]{1,2,0:T(8,128)S(1)} %add_sqrt_fusion, f32[]{:T(128)} %constant.29.clone.1), window={size=1x1x129 pad=0_0x0_0x64_64}, to_apply=%region_2.0 | reduce-window | flops 83886080 | bytes 5242884 | tf_op jit(solution)/shard_map/reduce_window | solution.py:18
  142.4 4.0 divide_convert_fusion.1
  146.4 10.4 %slice.38 = bf16[2,8,2560]{1,2,0:T(8,128)(2,1)} slice(bf16[2,128,2560]{1,2,0:T(8,128)(2,1)S(1)} %get-tuple-element.90), slice={[0:2:1], [0:128:16], [0:2560:1]} | slice | bytes 163840 | tf_op jit(solution)/shard_map/slice | solution.py:58
  156.8 10.2 %slice.39 = bf16[2,8,2560]{1,2,0:T(8,128)(2,1)} slice(bf16[2,128,2560]{1,2,0:T(8,128)(2,1)S(1)} %get-tuple-element.91), slice={[0:2:1], [0:128:16], [0:2560:1]} | slice | bytes 163840 | tf_op jit(solution)/shard_map/slice | solution.py:58
  167.0 3.8 maximum_bitcast_fusion
  170.8 3.5 copy.27
  177.1 11.7 %cosine_convert_fusion = (bf16[2560,256]{1,0:T(8,128)(2,1)S(1)}, bf16[2560,256]{1,0:T(8,128)(2,1)S(1)}) fusion(s32[256]{0:T(256)S(1)} %compare_select_fusion, s32[2560]{0:T(1024)S(1)} %iota_add_fusion), kind=kLoop, calls=%fused_computation.34 | loop fusion | flops 11141120 | bytes 2632704 | tf_op jit(solution)/shard_map/convert.9
  190.5 74.7 %all-gather.2.cloned.1.call-done = bf16[512,2,2,2560]{3,2,1,0:T(2,128)(2,1)} async-done(((bf16[8,2,2,2560]{3,2,1,0:T(2,128)(2,1)}), bf16[512,2,2,2560]{3,2,1,0:T(2,128)(2,1)}) %all-gather.2.cloned.1.call-update) | async-done | bytes 10485776 | tf_op jit(solution)/shard_map/all_gather | solution.py:63
  265.2 13.0 %reshape.97 = bf16[64,81920]{1,0:T(8,128)(2,1)} reshape(bf16[512,2,2,2560]{3,2,1,0:T(2,128)(2,1)} %all-gather.2.cloned.1.call-done) | data formatting | bytes 20971520 | tf_op jit(solution)/shard_map/reshape | solution.py:64
  278.2 13.8 %dot_general.11 = bf16[8,2,2,2560,64]{3,2,1,0,4:T(2,128)(2,1)} reshape(bf16[81920,64]{0,1:T(8,128)(2,1)} %bitcast.71) | data formatting | bytes 20971520 | tf_op jit(solution)/shard_map/dot_general | solution.py:65
  292.0 16.1 %fusion.8 = f32[4,8,2,2,2560]{4,0,3,2,1:T(4,128)} fusion(bf16[8,2,2,2560,64]{3,2,1,0,4:T(2,128)(2,1)} %dot_general.11, s32[64]{0:T(128)S(1)} %add_reduce_fusion, pred[64]{0:T(512)(128)(4,1)S(1)} %fusion.14), kind=kOutput, calls=%fused_computation.19 | convolution fusion | flops 41943552 | bytes 11796800 | tf_op jit(solution)/shard_map/dot_general | solution.py:65
  308.2 51.6 %while.10 = (s32[]{:T(128)}, f32[4,8,128,256]{3,2,1,0:T(8,128)}, f32[4,8,2,2,2560]{4,0,3,2,1:T(4,128)}, bf16[2,128,2560]{2,1,0:T(8,128)(2,1)S(1)}, bf16[2,128,25...) while((s32[]{:T(128)}, f32[4,8,128,256]{3,2,1,0:T(8,128)}, ...), condition=%wide.region_4.5_spmd, body=%wide.region_3.4_spmd.sunk | while | flops 2748841984 | bytes 53281388 | solution.py:88
  311.3 5.8 %add_convert_fusion.2 = (bf16[8,128,2560]{2,1,0:T(8,128)(2,1)S(1)}, bf16[8,128,2560]{2,1,0:T(8,128)(2,1)S(1)}) fusion(f32[128,2560]{1,0:T(8,128)S(1)} %get-tuple-element.145, f32[8,2560]{1,0:T(8,128)S(1)} %get-tuple-element.148, f32[128,2560]{1,0:T(8,128)S(1)} %get-tuple-element.149, f32[8,2560]{1,0:T(8,128)S(1)} %get-tuple-element.150, ...), kind=kLoop, calls=%fused_computation.5.clone.1 | loop fusion | flops 41943040 | bytes 16056320 | tf_op jit(solution)/shard_map/convert.7
  317.1 3.1 fusion.29
  324.1 5.8 %add_convert_fusion.2 = (bf16[8,128,2560]{2,1,0:T(8,128)(2,1)S(1)}, bf16[8,128,2560]{2,1,0:T(8,128)(2,1)S(1)}) fusion(f32[128,2560]{1,0:T(8,128)S(1)} %get-tuple-element.145, f32[8,2560]{1,0:T(8,128)S(1)} %get-tuple-element.148, f32[128,2560]{1,0:T(8,128)S(1)} %get-tuple-element.149, f32[8,2560]{1,0:T(8,128)S(1)} %get-tuple-element.150, ...), kind=kLoop, calls=%fused_computation.5.clone.1 | loop fusion | flops 41943040 | bytes 16056320 | tf_op jit(solution)/shard_map/convert.7
  329.9 3.1 fusion.29
  336.9 5.8 %add_convert_fusion.2 = (bf16[8,128,2560]{2,1,0:T(8,128)(2,1)S(1)}, bf16[8,128,2560]{2,1,0:T(8,128)(2,1)S(1)}) fusion(f32[128,2560]{1,0:T(8,128)S(1)} %get-tuple-element.145, f32[8,2560]{1,0:T(8,128)S(1)} %get-tuple-element.148, f32[128,2560]{1,0:T(8,128)S(1)} %get-tuple-element.149, f32[8,2560]{1,0:T(8,128)S(1)} %get-tuple-element.150, ...), kind=kLoop, calls=%fused_computation.5.clone.1 | loop fusion | flops 41943040 | bytes 16056320 | tf_op jit(solution)/shard_map/convert.7
  342.7 3.1 fusion.29
  349.8 5.8 %add_convert_fusion.2 = (bf16[8,128,2560]{2,1,0:T(8,128)(2,1)S(1)}, bf16[8,128,2560]{2,1,0:T(8,128)(2,1)S(1)}) fusion(f32[128,2560]{1,0:T(8,128)S(1)} %get-tuple-element.145, f32[8,2560]{1,0:T(8,128)S(1)} %get-tuple-element.148, f32[128,2560]{1,0:T(8,128)S(1)} %get-tuple-element.149, f32[8,2560]{1,0:T(8,128)S(1)} %get-tuple-element.150, ...), kind=kLoop, calls=%fused_computation.5.clone.1 | loop fusion | flops 41943040 | bytes 16056320 | tf_op jit(solution)/shard_map/convert.7
  355.6 3.1 fusion.29
  359.8 94.6 %all-reduce.2.cloned.1.call-done = f32[4,8,128,256]{3,2,1,0:T(8,128)} async-done(((f32[4,8,128,256]{3,2,1,0:T(8,128)}), f32[4,8,128,256]{3,2,1,0:T(8,128)}) %all-reduce.2.cloned.1.call-update) | async-done | bytes 4194320 | tf_op jit(solution)/shard_map/psum | solution.py:89
  454.4 2.3 constant_dynamic-slice_fusion.1
  (60 shorter events, 21.1 us)
Async XLA Ops:
  6.5 258.7 %all-gather.2.cloned.1.call-start = ((), (), s32[]{:S(2)}) async-start(), calls=%async_computation | async-start | bytes 10649600 | tf_op jit(solution)/shard_map/all_gather | solution.py:63
  10.1 2.3 copy-start
  146.4 20.6 %copy-start.1 = (bf16[2,128,2560]{1,2,0:T(8,128)(2,1)}, bf16[2,128,2560]{1,2,0:T(8,128)(2,1)S(1)}, u32[]{:S(2)}) copy-start(bf16[2,128,2560]{1,2,0:T(8,128)(2,1)S(1)} %get-tuple-element.91) | copy-start | bytes 3932164
  174.4 280.0 %all-reduce.2.cloned.1.call-start = ((), (), s32[]{:S(2)}) async-start(), calls=%async_computation.1 | async-start | bytes 8388608 | tf_op jit(solution)/shard_map/psum | solution.py:89
  174.4 2.3 copy-start.3
  174.4 2.3 copy-start.4
  311.3 5.8 %copy-start.2 = (bf16[5120,256]{1,0:T(8,128)(2,1)S(1)}, bf16[5120,256]{1,0:T(8,128)(2,1)}, u32[]{:S(2)}) copy-start(bf16[5120,256]{1,0:T(8,128)(2,1)} %get-tuple-element.178) | copy-start | bytes 7864324 | tf_op jit(solution)/shard_map/while
  324.1 5.8 %copy-start.2 = (bf16[5120,256]{1,0:T(8,128)(2,1)S(1)}, bf16[5120,256]{1,0:T(8,128)(2,1)}, u32[]{:S(2)}) copy-start(bf16[5120,256]{1,0:T(8,128)(2,1)} %get-tuple-element.178) | copy-start | bytes 7864324 | tf_op jit(solution)/shard_map/while
  336.9 5.8 %copy-start.2 = (bf16[5120,256]{1,0:T(8,128)(2,1)S(1)}, bf16[5120,256]{1,0:T(8,128)(2,1)}, u32[]{:S(2)}) copy-start(bf16[5120,256]{1,0:T(8,128)(2,1)} %get-tuple-element.178) | copy-start | bytes 7864324 | tf_op jit(solution)/shard_map/while
  349.7 5.8 %copy-start.2 = (bf16[5120,256]{1,0:T(8,128)(2,1)S(1)}, bf16[5120,256]{1,0:T(8,128)(2,1)}, u32[]{:S(2)}) copy-start(bf16[5120,256]{1,0:T(8,128)(2,1)} %get-tuple-element.178) | copy-start | bytes 7864324 | tf_op jit(solution)/shard_map/while
Sparse Core Ops, SparseCore 0:
  174.5 90.6 all-gather.1
  359.9 94.4 all-reduce.1
where the time goes:
time: 467 us; the launch traced here: 464 us
  other arithmetic  178 us (38%)
  waiting for transfers between devices  169 us (36%)
  local copies, waits for them, and re-layouts  73.9 us (16%)
  matrix products  28.4 us (6%)
  between operations  14.1 us (3%)
    another operation x1, other arithmetic, whiten(): lax.reduce_window(amplitude, jnp.zeros((), amplitude.dtype), lax.add, win...  129 us
    psum x1, waiting for transfers between devices, shards(): summed_hours = lax.psum(partial_stacks, 'hour')  94.6 us
    all_gather x1, waiting for transfers between devices, shards(): gathered = lax.all_gather(local_sources, 'chan', axis=0, tiled=True)  74.7 us
    another operation x6, other arithmetic  34.9 us
    dot_general x1, matrix products, shards(): chosen = jnp.dot(onehot, flattened, preferred_element_type=jnp.float32)  16.1 us
    dot_general x1, local copies, waits for them, and re-layouts, shards(): chosen = jnp.dot(onehot, flattened, preferred_element_type=jnp.float32)  13.8 us
    reshape x1, local copies, waits for them, and re-layouts, shards(): flattened = gathered.reshape(block_count, -1)  13 us
    dot_general x4, matrix products, one_slot(): jnp.dot(cross, table_values, preferred_element_type=jnp.float32)  12.3 us
  transfers between devices with their start and end apart: 2, of which 2 were waited for; matrix products, arithmetic and copies ran while one was open for 3% of the time, Pallas kernels for 0%

commit v1 on v0

--- a/solution.py
+++ b/solution.py
@@ -60,7 +60,8 @@
     receiver = lax.axis_index("chan")
     onehot = slot_onehot(partner_lists, partner_counts, receiver).astype(jnp.bfloat16)
     slot_total = onehot.shape[0]
-    gathered = lax.all_gather(local_sources, "chan", axis=0, tiled=True)
+    repeated = jnp.stack([local_sources] * lax.axis_size("chan"))
+    gathered = jnp.concatenate(lax.all_to_all(repeated, "chan", 0, 0), axis=0)
     flattened = gathered.reshape(block_count, -1)
     chosen = jnp.dot(onehot, flattened, preferred_element_type=jnp.float32)
     chosen = chosen.reshape(slot_total, VS, windows, 2, band_bins)

time: 467 us -> 624 us (1.34)
  waiting for transfers between devices: 169 us -> 309 us
  starting transfers between devices: 0.04 us -> 13.4 us
  local copies, waits for them, and re-layouts: 73.9 us -> 80.7 us
    all_to_all x0 -> x1, waiting for transfers between devices: none -> 215 us  [shards(): gathered = jnp.concatenate(lax.all_to_all(repeated, 'chan', 0, 0), axis=0)]
    all_gather x1 -> x0, waiting for transfers between devices: 74.7 us -> none  [shards(): gathered = lax.all_gather(local_sources, 'chan', axis=0, tiled=True)]
    another operation x0 -> x4, local copies, waits for them, and re-layouts: none -> 23.2 us  [the longest x1 13 us: shards(): flattened = gathered.reshape(block_count, -1)]
    all_to_all x0 -> x1, starting transfers between devices: none -> 13.3 us  [shards(): gathered = jnp.concatenate(lax.all_to_all(repeated, 'chan', 0, 0), axis=0)]
    reshape x1 -> x0, local copies, waits for them, and re-layouts: 13 us -> none  [shards(): flattened = gathered.reshape(block_count, -1)]
where the time goes in v1:
time: 624 us; the launch traced here: 621 us
  waiting for transfers between devices  309 us (50%)
  other arithmetic  175 us (28%)
  local copies, waits for them, and re-layouts  80.7 us (13%)
  matrix products  28.4 us (5%)
  between operations  14.1 us (2%)
  starting transfers between devices  13.4 us (2%)
    all_to_all x1, waiting for transfers between devices, shards(): gathered = jnp.concatenate(lax.all_to_all(repeated, 'chan', 0, 0), axis=0)  215 us
    another operation x1, other arithmetic, whiten(): lax.reduce_window(amplitude, jnp.zeros((), amplitude.dtype), lax.add, win...  130 us
    psum x1, waiting for transfers between devices, shards(): summed_hours = lax.psum(partial_stacks, 'hour')  94.8 us
    another operation x6, other arithmetic  34.9 us
    dot_general x1, matrix products, shards(): chosen = jnp.dot(onehot, flattened, preferred_element_type=jnp.float32)  16.1 us
    dot_general x1, local copies, waits for them, and re-layouts, shards(): chosen = jnp.dot(onehot, flattened, preferred_element_type=jnp.float32)  13.8 us
    all_to_all x1, starting transfers between devices, shards(): gathered = jnp.concatenate(lax.all_to_all(repeated, 'chan', 0, 0), axis=0)  13.3 us
    another operation x1, local copies, waits for them, and re-layouts, shards(): flattened = gathered.reshape(block_count, -1)  13 us
  transfers between devices with their start and end apart: 2, of which 2 were waited for; matrix products, arithmetic and copies ran while one was open for 3% of the time, Pallas kernels for 0%

profile of v1, /device:TPU:1, one launch (start us, length us, event | category | flops | bytes accessed | tf_op | source)
XLA Modules:
  0.0 621.3 jit_solution(1930923919226341317)
XLA Ops:
  6.5 3.2 copy.18
  10.1 2.3 copy-done
  13.3 129.9 %reduce_window.7 = f32[2,128,2560]{1,2,0:T(8,128)} reduce-window(f32[2,128,2560]{1,2,0:T(8,128)S(1)} %add_sqrt_fusion, f32[]{:T(128)} %constant.29.clone.1), window={size=1x1x129 pad=0_0x0_0x64_64}, to_apply=%region_2.0 | reduce-window | flops 83886080 | bytes 5242884 | tf_op jit(solution)/shard_map/reduce_window | solution.py:18
  143.2 4.0 divide_convert_fusion.1
  147.1 10.4 %slice.38 = bf16[2,8,2560]{1,2,0:T(8,128)(2,1)} slice(bf16[2,128,2560]{1,2,0:T(8,128)(2,1)S(1)} %get-tuple-element.84), slice={[0:2:1], [0:128:16], [0:2560:1]} | slice | bytes 163840 | tf_op jit(solution)/shard_map/slice | solution.py:58
  159.3 10.2 %slice.39 = bf16[2,8,2560]{1,2,0:T(8,128)(2,1)} slice(bf16[2,128,2560]{1,2,0:T(8,128)(2,1)S(1)} %get-tuple-element.85), slice={[0:2:1], [0:128:16], [0:2560:1]} | slice | bytes 163840 | tf_op jit(solution)/shard_map/slice | solution.py:58
  171.4 6.8 %stack.11 = bf16[64,8,2,2,2560]{4,3,2,1,0:T(2,128)(2,1)} broadcast(bf16[8,2,2,2560]{3,2,1,0:T(2,128)(2,1)S(1)} %copy.21), dimensions={1,2,3,4} | broadcast | bytes 10649600 | tf_op jit(solution)/shard_map/stack | solution.py:63
  178.2 13.3 %all-to-all-start = ((bf16[64,8,2,2,2560]{4,3,2,1,0:T(2,128)(2,1)}), bf16[64,8,2,2,2560]{4,3,2,1,0:T(2,128)(2,1)}, u32[]{:S(2)}, u32[]{:S(2)}) async-start(bf16[64,8,2,2,2560]{4,3,2,1,0:T(2,128)(2,1)} %stack.11), calls=%async_computation | async-start | bytes 20971520 | tf_op jit(solution)/shard_map/all_to_all | solution.py:64
  194.2 11.7 %cosine_convert_fusion = (bf16[2560,256]{1,0:T(8,128)(2,1)S(1)}, bf16[2560,256]{1,0:T(8,128)(2,1)S(1)}) fusion(s32[256]{0:T(256)S(1)} %compare_select_fusion, s32[2560]{0:T(1024)S(1)} %iota_add_fusion), kind=kLoop, calls=%fused_computation.33 | loop fusion | flops 11141120 | bytes 2632704 | tf_op jit(solution)/shard_map/convert.9
  207.6 214.6 %all-to-all-done = bf16[64,8,2,2,2560]{4,3,2,1,0:T(2,128)(2,1)} async-done(((bf16[64,8,2,2,2560]{4,3,2,1,0:T(2,128)(2,1)}), bf16[64,8,2,2,2560]{4,3,2,1,0:T(2,128)(2,1)}, u32[]{:S(2)}, u32[]{:S(2)}) %all-to-all-start) | async-done | bytes 10485792 | tf_op jit(solution)/shard_map/all_to_all | solution.py:64
  422.3 13.0 %reshape_reshape.3 = bf16[64,81920]{1,0:T(8,128)(2,1)} reshape(bf16[64,8,2,2,2560]{4,3,2,1,0:T(2,128)(2,1)} %all-to-all-done) | data formatting | bytes 20971520 | tf_op jit(solution)/shard_map/reshape;reshape | solution.py:65
  435.2 13.8 %dot_general.11 = bf16[8,2,2,2560,64]{3,2,1,0,4:T(2,128)(2,1)} reshape(bf16[81920,64]{0,1:T(8,128)(2,1)} %bitcast.71) | data formatting | bytes 20971520 | tf_op jit(solution)/shard_map/dot_general | solution.py:66
  449.1 16.1 %fusion.8 = f32[4,8,2,2,2560]{4,0,3,2,1:T(4,128)} fusion(bf16[8,2,2,2560,64]{3,2,1,0,4:T(2,128)(2,1)} %dot_general.11, s32[64]{0:T(128)S(1)} %add_reduce_fusion, pred[64]{0:T(512)(128)(4,1)S(1)} %fusion.14), kind=kOutput, calls=%fused_computation.19 | convolution fusion | flops 41943552 | bytes 11796800 | tf_op jit(solution)/shard_map/dot_general | solution.py:66
  465.2 51.5 %while.10 = (s32[]{:T(128)}, f32[4,8,128,256]{3,2,1,0:T(8,128)}, f32[4,8,2,2,2560]{4,0,3,2,1:T(4,128)}, bf16[2,128,2560]{2,1,0:T(8,128)(2,1)S(1)}, bf16[2,128,25...) while((s32[]{:T(128)}, f32[4,8,128,256]{3,2,1,0:T(8,128)}, ...), condition=%wide.region_4.5_spmd, body=%wide.region_3.4_spmd.sunk | while | flops 2748841984 | bytes 53281388 | solution.py:89
  468.4 5.8 add_convert_fusion.2
  474.2 3.1 fusion.29
  481.2 5.8 add_convert_fusion.2
  487.0 3.1 fusion.29
  494.0 5.8 add_convert_fusion.2
  499.8 3.1 fusion.29
  506.8 5.8 add_convert_fusion.2
  512.6 3.1 fusion.29
  516.8 94.8 %all-reduce.2.cloned.1.call-done = f32[4,8,128,256]{3,2,1,0:T(8,128)} async-done(((f32[4,8,128,256]{3,2,1,0:T(8,128)}), f32[4,8,128,256]{3,2,1,0:T(8,128)}) %all-reduce.2.cloned.1.call-update) | async-done | bytes 4194320 | tf_op jit(solution)/shard_map/psum | solution.py:90
  611.6 2.3 constant_dynamic-slice_fusion.1
  (62 shorter events, 24.6 us)
Async XLA Ops:
  10.1 2.3 copy-start
  147.1 22.4 %copy-start.1 = (bf16[2,128,2560]{1,2,0:T(8,128)(2,1)}, bf16[2,128,2560]{1,2,0:T(8,128)(2,1)S(1)}, u32[]{:S(2)}) copy-start(bf16[2,128,2560]{1,2,0:T(8,128)(2,1)S(1)} %get-tuple-element.85) | copy-start | bytes 3932164
  178.2 244.1 %all-to-all-start = ((bf16[64,8,2,2,2560]{4,3,2,1,0:T(2,128)(2,1)}), bf16[64,8,2,2,2560]{4,3,2,1,0:T(2,128)(2,1)}, u32[]{:S(2)}, u32[]{:S(2)}) async-start(bf16[64,8,2,2,2560]{4,3,2,1,0:T(2,128)(2,1)} %stack.11), calls=%async_computation | async-start | bytes 20971520 | tf_op jit(solution)/shard_map/all_to_all | solution.py:64
  191.5 420.1 %all-reduce.2.cloned.1.call-start = ((), (), s32[]{:S(2)}) async-start(), calls=%async_computation.1 | async-start | bytes 8388608 | tf_op jit(solution)/shard_map/psum | solution.py:90
  191.6 2.3 copy-start.3
  191.6 2.3 copy-start.4
  468.4 5.8 copy-start.2
  481.2 5.8 copy-start.2
  494.0 5.8 copy-start.2
  506.8 5.8 copy-start.2
Sparse Core Ops, SparseCore 0:
  516.9 94.6 all-reduce.1
